TPU v7x, 32 devices: a whole 2x2x4 slice. The times are simulated.
32 devices in a mesh: groups: 2 (over y), ulysses: 8 (over z, x), seq: 2 (over core).
Axes of the slice: x: 2, y: 2, z: 4, core: 2. Of those that a mesh axis runs over, the one named last changes fastest.
Arguments:
- query_states: bfloat16 [2048, 8192], P(('groups', 'ulysses', 'seq')), parts along dimension 0, may hold values from -6 to 6
- key_states: bfloat16 [2048, 1024], P(('groups', 'ulysses', 'seq')), parts along dimension 0, may hold values from -6 to 6
- value_states: bfloat16 [2048, 1024], P(('groups', 'ulysses', 'seq')), parts along dimension 0, may hold values from -6 to 6
- turn_ids: int32 [2048], P('groups'), parts along dimension 0, may hold values from 0 to 3, never falling along the last dimension, each value on 1 to 512 neighbouring positions
- judge_positions: int32 [256], P('groups'), parts along dimension 0, may hold values from 0 to 1023, as said below
Outputs:
- attended_states: bfloat16 [2048, 8192], P(('groups', 'ulysses', 'seq')), parts along dimension 0
There are 2 independent parts, one for each index of `groups`. A program takes and returns all parts, laid end to end along the dimension named above; each array names one. Nothing has to cross between parts.
Inputs may be any that keep to these rules, and one draw needn't show every extreme that they name: `turn_ids`: turn numbers never fall along the conversation; every turn spans 1 to 512 tokens, one exactly that many. `judge_positions`: distinct positions, 0 and 1023 among them.
All inputs are finite; a program needn't handle non-finite values.
Results may differ from a plain program's by a relative error of at most 0.004.
Values may be sent and summed in bfloat16 or wider, within the bound.
No kernel may reach another device: no remote copies, remote signals or barrier semaphores. Data moves between devices by JAX's collectives and lax.ppermute only.
A program may use at most 64 MiB of HBM per device.

v0:
```python
import math
import jax
import jax.numpy as jnp
from jax import lax
from jax.sharding import PartitionSpec as P

HEAD_DIM = 128
floor_score = -1e30


def absorb(
    carried,
    query_block,
    query_place,
    query_turn,
    keys_block,
    values_block,
    keys_place,
    keys_turn,
    keys_judge,
    scaling,
):
    maxima, totals, running = carried
    scores = (
        jnp.einsum("qhd,kd->qhk", query_block, keys_block, preferred_element_type=jnp.float32)
        * scaling
    )
    visible = (keys_place[None, :] <= query_place[:, None]) & (
        (keys_turn[None, :] == query_turn[:, None]) | keys_judge[None, :]
    )
    scores = jnp.where(visible[:, None, :], scores, floor_score)
    newest = jnp.maximum(maxima, jnp.max(scores, axis=2))
    factor = jnp.exp(maxima - newest)
    weights = jnp.exp(scores - newest[:, :, None])
    totals = totals * factor + jnp.sum(weights, axis=2)
    running = running * factor[:, :, None] + jnp.einsum(
        "qhk,kd->qhd",
        weights.astype(jnp.bfloat16),
        values_block,
        preferred_element_type=jnp.float32,
    )
    return (newest, totals, running)


def attend(
    carried,
    queries,
    query_place,
    query_turn,
    key_rows,
    value_rows,
    keys_place,
    keys_turn,
    keys_judge,
    scaling,
):
    query_count = queries.shape[0]
    key_count = key_rows.shape[0]
    query_step = math.gcd(query_count, 512)
    key_step = math.gcd(key_count, 512)

    def over_queries(row_index, totals_all):
        offset = row_index * query_step
        query_block = lax.dynamic_slice_in_dim(queries, offset, query_step, 0)
        block_place = lax.dynamic_slice_in_dim(query_place, offset, query_step, 0)
        block_turn = lax.dynamic_slice_in_dim(query_turn, offset, query_step, 0)
        window = tuple(
            (lax.dynamic_slice_in_dim(member, offset, query_step, 0) for member in totals_all)
        )

        def over_keys(key_index, current):
            key_offset = key_index * key_step
            keys_block = lax.dynamic_slice_in_dim(key_rows, key_offset, key_step, 0)
            values_block = lax.dynamic_slice_in_dim(value_rows, key_offset, key_step, 0)
            block_keys_place = lax.dynamic_slice_in_dim(keys_place, key_offset, key_step, 0)
            block_keys_turn = lax.dynamic_slice_in_dim(keys_turn, key_offset, key_step, 0)
            block_keys_judge = lax.dynamic_slice_in_dim(keys_judge, key_offset, key_step, 0)
            return lax.cond(
                jnp.max(block_place) >= jnp.min(block_keys_place),
                lambda inside: absorb(
                    inside,
                    query_block,
                    block_place,
                    block_turn,
                    keys_block,
                    values_block,
                    block_keys_place,
                    block_keys_turn,
                    block_keys_judge,
                    scaling,
                ),
                lambda inside: inside,
                current,
            )

        window = lax.fori_loop(0, key_count // key_step, over_keys, window)
        return tuple(
            (
                lax.dynamic_update_slice_in_dim(member, updated, offset, 0)
                for member, updated in zip(totals_all, window)
            )
        )

    return lax.fori_loop(0, query_count // query_step, over_queries, carried)


def spread(array, copies):
    row_count = array.shape[0]
    shared_heads = array.shape[1] // HEAD_DIM
    widened = jnp.broadcast_to(
        array.reshape(row_count, shared_heads, 1, HEAD_DIM),
        (row_count, shared_heads, copies // shared_heads, HEAD_DIM),
    )
    return widened.reshape(row_count, copies, HEAD_DIM)


def shards(query_states, key_states, value_states, turn_ids, judge_positions):
    tokens_here = query_states.shape[0]
    ulysses_count = lax.axis_size("ulysses")
    stripe_count = lax.axis_size("seq")
    stripe = lax.axis_index("seq")
    heads_here = query_states.shape[1] // HEAD_DIM // ulysses_count
    seq_total = tokens_here * ulysses_count * stripe_count
    scaling = 1.0 / math.sqrt(HEAD_DIM)
    positions = jnp.arange(seq_total, dtype=jnp.int32)
    judged = jnp.any(positions[:, None] == judge_positions[None, :], axis=1)
    exchanged = lax.all_to_all(
        query_states.reshape(tokens_here, ulysses_count, heads_here * HEAD_DIM),
        "ulysses",
        split_axis=1,
        concat_axis=0,
        tiled=True,
    )
    query_total = ulysses_count * tokens_here
    queries = exchanged.reshape(query_total, heads_here, HEAD_DIM)
    local_rows = jnp.arange(query_total, dtype=jnp.int32)
    query_place = (
        local_rows // tokens_here * stripe_count + stripe
    ) * tokens_here + local_rows % tokens_here
    query_turn = jnp.take(turn_ids, query_place)
    carried = (
        jnp.full((query_total, heads_here), floor_score, jnp.float32),
        jnp.zeros((query_total, heads_here), jnp.float32),
        jnp.zeros((query_total, heads_here, HEAD_DIM), jnp.float32),
    )
    keys_out, values_out = (
        lax.all_to_all(
            spread(key_states, ulysses_count), "ulysses", split_axis=1, concat_axis=0, tiled=True
        ),
        lax.all_to_all(
            spread(value_states, ulysses_count), "ulysses", split_axis=1, concat_axis=0, tiled=True
        ),
    )
    key_rows = keys_out.reshape(query_total, HEAD_DIM)
    value_rows = values_out.reshape(query_total, HEAD_DIM)
    pieces = (
        lax.all_gather(key_rows, "seq", axis=0, tiled=True),
        lax.all_gather(value_rows, "seq", axis=0, tiled=True),
    )
    piece_rows = pieces[0].shape[0]
    gathered_rows = jnp.arange(piece_rows, dtype=jnp.int32)
    source_stripe = gathered_rows // query_total
    within = gathered_rows % query_total
    key_place = (
        within // tokens_here * stripe_count + source_stripe
    ) * tokens_here + within % tokens_here
    maxima, totals, running = attend(
        carried,
        queries,
        query_place,
        query_turn,
        pieces[0],
        pieces[1],
        key_place,
        jnp.take(turn_ids, key_place),
        jnp.take(judged, key_place),
        scaling,
    )
    result = (
        (running / totals[:, :, None])
        .astype(jnp.bfloat16)
        .reshape(query_total, 1, heads_here * HEAD_DIM)
    )
    returned = lax.all_to_all(result, "ulysses", split_axis=0, concat_axis=1, tiled=True)
    return returned.reshape(tokens_here, ulysses_count * heads_here * HEAD_DIM)


def solution(mesh):
    placed = (
        P(("groups", "ulysses", "seq"), None),
        P(("groups", "ulysses", "seq"), None),
        P(("groups", "ulysses", "seq"), None),
        P("groups"),
        P("groups"),
    )
    return jax.shard_map(
        shards,
        mesh=mesh,
        in_specs=placed,
        out_specs=P(("groups", "ulysses", "seq"), None),
        check_vma=False,
    )
```

profile of v0, /device:TPU:0, one launch (start us, length us, event | category | flops | bytes accessed | tf_op | source)
XLA Modules:
  0.0 126.2 jit_solution(8405274671733121284)
XLA Ops:
  1.6 7.3 %all-to-all-start = ((bf16[64,8,128]{2,0,1:T(8,128)(2,1)}), bf16[64,8,128]{2,0,1:T(8,128)(2,1)S(1)}, u32[]{:S(2)}, u32[]{:S(2)}) async-start(bf16[64,8,128]{2,0,1:T(8,128)(2,1)} %copy_bitcast_fusion.2), calls=%async_computation | async-start | bytes 262144 | tf_op jit(solution)/shard_map/all_to_all | solution.py:147
  10.4 5.8 %all-to-all-done = bf16[64,8,128]{2,0,1:T(8,128)(2,1)S(1)} async-done(((bf16[64,8,128]{2,0,1:T(8,128)(2,1)}), bf16[64,8,128]{2,0,1:T(8,128)(2,1)S(1)}, u32[]{:S(2)}, u32[]{:S(2)}) %all-to-all-start) | async-done | bytes 131104 | tf_op jit(solution)/shard_map/all_to_all | solution.py:147
  16.2 3.4 %all-to-all-start.2 = ((bf16[64,8,128]{2,0,1:T(8,128)(2,1)}), bf16[64,8,128]{2,0,1:T(8,128)(2,1)S(1)}, u32[]{:S(2)}, u32[]{:S(2)}) async-start(bf16[64,8,128]{2,0,1:T(8,128)(2,1)} %copy_bitcast_fusion.1), calls=%async_computation.2 | async-start | bytes 262144 | tf_op jit(solution)/shard_map/all_to_all | solution.py:150
  19.6 2.3 %copy.51 = bf16[8,8,8,1024]{3,2,0,1:T(8,128)(2,1)} copy(bf16[8,8,8,1024]{3,2,1,0:T(8,128)(2,1)} %bitcast.71) | data formatting | bytes 2097152 | tf_op jit(solution)/shard_map/reshape | solution.py:128
  21.9 5.0 %all-to-all-done.2 = bf16[64,8,128]{2,0,1:T(8,128)(2,1)S(1)} async-done(((bf16[64,8,128]{2,0,1:T(8,128)(2,1)}), bf16[64,8,128]{2,0,1:T(8,128)(2,1)S(1)}, u32[]{:S(2)}, u32[]{:S(2)}) %all-to-all-start.2) | async-done | bytes 131104 | tf_op jit(solution)/shard_map/all_to_all | solution.py:150
  26.9 3.6 %all-to-all-start.1 = ((bf16[64,8,1024]{2,0,1:T(8,128)(2,1)}), bf16[64,8,1024]{2,0,1:T(8,128)(2,1)S(1)}, u32[]{:S(2)}, u32[]{:S(2)}) async-start(bf16[64,8,1024]{2,0,1:T(8,128)(2,1)} %bitcast.66), calls=%async_computation.1 | async-start | bytes 2097152 | tf_op jit(solution)/shard_map/all_to_all | solution.py:127
  30.5 5.7 %gather_fusion = s32[1024]{0:T(1024)S(1)} fusion(s32[1024]{0:T(1024)} %param.12, s32[1024]{0:T(1024)S(1)} %broadcast_clamp_fusion), kind=kCustom, calls=%fused_computation | custom fusion | bytes 12288 | tf_op jit(solution)/shard_map/jit(_take)/gather | solution.py:175
  36.3 2.3 %gather_fusion.1 = s32[512]{0:T(512)S(1)} fusion(s32[1024]{0:T(1024)S(1)} %copy-done.1, s32[1024]{0:T(1024)S(1)} %pad_clamp_fusion), kind=kCustom, calls=%fused_computation.1 | custom fusion | bytes 6144 | tf_op jit(solution)/shard_map/jit(_take)/gather | solution.py:140
  38.8 6.8 %gather_fusion.2 = pred[1024]{0:T(1024)(128)(4,1)S(1)} fusion(pred[1024]{0:T(1024)(128)(4,1)S(1)} %fusion.24, s32[1024]{0:T(1024)S(1)} %broadcast_clamp_fusion), kind=kCustom, calls=%fused_computation.2 | custom fusion | bytes 6144 | tf_op jit(solution)/shard_map/jit(_take)/gather | solution.py:176
  48.1 2.0 %all_gather.6 = bf16[1024,128]{1,0:T(8,128)(2,1)S(1)} all-gather(bf16[512,128]{1,0:T(8,128)(2,1)S(1)} %bitcast.72), channel_id=1, replica_groups=mesh['groups'=2,'ulysses'=8,'seq'=2] {'seq'}, dimensions={0}, use_global_device_ids=true | all-gather | bytes 393216 | tf_op jit(solution)/shard_map/all_gather | solution.py:157
  50.1 2.1 %all_gather.7 = bf16[1024,128]{1,0:T(8,128)(2,1)} all-gather(bf16[512,128]{1,0:T(8,128)(2,1)S(1)} %bitcast.73), channel_id=1, replica_groups=mesh['groups'=2,'ulysses'=8,'seq'=2] {'seq'}, dimensions={0}, use_global_device_ids=true | all-gather | bytes 393216 | tf_op jit(solution)/shard_map/all_gather | solution.py:158
  52.2 1.9 %all-to-all-done.1 = bf16[64,8,1024]{2,0,1:T(8,128)(2,1)S(1)} async-done(((bf16[64,8,1024]{2,0,1:T(8,128)(2,1)}), bf16[64,8,1024]{2,0,1:T(8,128)(2,1)S(1)}, u32[]{:S(2)}, u32[]{:S(2)}) %all-to-all-start.1) | async-done | bytes 1048608 | tf_op jit(solution)/shard_map/all_to_all | solution.py:127
  55.2 31.6 %while.31 = (s32[]{:T(128)}, f32[512,8]{0,1:T(8,128)S(1)}, f32[512,8]{0,1:T(8,128)}, f32[512,8,128]{2,0,1:T(8,128)S(1)}, s32[1024]{0:T(1024)}, /*index=5*/s32[]{...) while((s32[]{:T(128)}, f32[512,8]{0,1:T(8,128)S(1)}, ...), condition=%wide.region_8.9_spmd.clone, body=%wide.region_2.8_spmd.clone.sunk | while | flops 1098925056 | bytes 33209420 | solution.py:96
  55.2 2.0 %fusion.67 = (s32[]{:T(128)}, s32[512]{0:T(512)}) fusion(s32[1024]{0:T(1024)} %get-tuple-element.768, s32[]{:T(128)} %select_n.391), kind=kLoop, calls=%fused_computation.117.clone.1 | loop fusion | flops 511 | bytes 4104 | tf_op jit(solution)/shard_map/while/body/eval_jaxpr/while/body/eval_jaxpr/reduce_min | solution.py:79
  61.5 9.5 %conditional.3 = ((f32[512,8]{0,1:T(8,128)S(1)}, f32[512,8]{0,1:T(8,128)}, f32[512,8,128]{2,0,1:T(8,128)S(1)})) conditional(s32[]{:T(128)} %convert_element_type.25, (f32[512,8]{0,1:T(8,128)S(1)}, f32[512,8]{0,1:T(8,128)}, f32[512,8,128]{2,0,1:T(8,128)S(1)}) %tuple.76, (s32[512]{0:T(512)}, s32[512]{0:T(512)}, s32[1024]{0:T(1024)}, s32[]{:T(128)}, ...), branch_computations={%region_4.4_spmd, %region_5.7_spmd.clone} | conditional | flops 1098922496 | bytes 33194124 | solution.py:78
  66.3 1.7 %fusion.3 = f32[512,8]{0,1:T(8,128)S(1)} fusion(f32[512,512,8]{1,0,2:T(8,128)S(1)} %get-tuple-element.622, f32[512,8]{0,1:T(8,128)S(1)} %max.5, pred[512,512]{0,1:T(8,128)(4,1)S(1)} %or_and_fusion), kind=kLoop, calls=%fused_computation.7 | loop fusion | flops 8384512 | bytes 8683520 | tf_op jit(solution)/shard_map/while/body/eval_jaxpr/while/body/eval_jaxpr/cond/branch_1_fun/reduce_sum | solution.py:35
  68.1 2.8 %multiply_add_fusion = f32[512,8,128]{2,0,1:T(8,128)S(1)} fusion(f32[512,8,128]{2,0,1:T(8,128)S(1)} %get-tuple-element.554, f32[512,512,8]{1,0,2:T(8,128)S(1)} %get-tuple-element.622, f32[512,8]{0,1:T(8,128)S(1)} %max.5, pred[512,512]{0,1:T(8,128)(4,1)S(1)} %or_and_fusion, f32[512,8]{0,1:T(8,128)S(1)} %get-tuple-element.618, ...), kind=kOutput, calls=%fused_computation.11 | convolution fusion | flops 546308096 | bytes 13008900 | tf_op jit(solution)/shard_map/while/body/eval_jaxpr/while/body/eval_jaxpr/cond/branch_1_fun/qhk,kd->qhd/dot_general | solution.py:36
  71.0 2.0 %fusion.67 = (s32[]{:T(128)}, s32[512]{0:T(512)}) fusion(s32[1024]{0:T(1024)} %get-tuple-element.768, s32[]{:T(128)} %select_n.391), kind=kLoop, calls=%fused_computation.117.clone.1 | loop fusion | flops 511 | bytes 4104 | tf_op jit(solution)/shard_map/while/body/eval_jaxpr/while/body/eval_jaxpr/reduce_min | solution.py:79
  77.3 9.5 %conditional.3 = ((f32[512,8]{0,1:T(8,128)S(1)}, f32[512,8]{0,1:T(8,128)}, f32[512,8,128]{2,0,1:T(8,128)S(1)})) conditional(s32[]{:T(128)} %convert_element_type.25, (f32[512,8]{0,1:T(8,128)S(1)}, f32[512,8]{0,1:T(8,128)}, f32[512,8,128]{2,0,1:T(8,128)S(1)}) %tuple.76, (s32[512]{0:T(512)}, s32[512]{0:T(512)}, s32[1024]{0:T(1024)}, s32[]{:T(128)}, ...), branch_computations={%region_4.4_spmd, %region_5.7_spmd.clone} | conditional | flops 1098922496 | bytes 33194124 | solution.py:78
  82.1 1.7 %fusion.3 = f32[512,8]{0,1:T(8,128)S(1)} fusion(f32[512,512,8]{1,0,2:T(8,128)S(1)} %get-tuple-element.622, f32[512,8]{0,1:T(8,128)S(1)} %max.5, pred[512,512]{0,1:T(8,128)(4,1)S(1)} %or_and_fusion), kind=kLoop, calls=%fused_computation.7 | loop fusion | flops 8384512 | bytes 8683520 | tf_op jit(solution)/shard_map/while/body/eval_jaxpr/while/body/eval_jaxpr/cond/branch_1_fun/reduce_sum | solution.py:35
  83.9 2.8 %multiply_add_fusion = f32[512,8,128]{2,0,1:T(8,128)S(1)} fusion(f32[512,8,128]{2,0,1:T(8,128)S(1)} %get-tuple-element.554, f32[512,512,8]{1,0,2:T(8,128)S(1)} %get-tuple-element.622, f32[512,8]{0,1:T(8,128)S(1)} %max.5, pred[512,512]{0,1:T(8,128)(4,1)S(1)} %or_and_fusion, f32[512,8]{0,1:T(8,128)S(1)} %get-tuple-element.618, ...), kind=kOutput, calls=%fused_computation.11 | convolution fusion | flops 546308096 | bytes 13008900 | tf_op jit(solution)/shard_map/while/body/eval_jaxpr/while/body/eval_jaxpr/cond/branch_1_fun/qhk,kd->qhd/dot_general | solution.py:36
  86.8 1.9 %copy.37 = f32[512,8,128]{0,2,1:T(8,128)} copy(f32[512,8,128]{2,0,1:T(8,128)S(1)} %get-tuple-element.428) | data formatting | bytes 4194304 | tf_op jit(solution)/shard_map/while/body/eval_jaxpr/while | solution.py:96
  88.7 1.9 %divide_convert_fusion = bf16[512,8,128]{0,2,1:T(8,128)(2,1)S(1)} fusion(f32[512,8,128]{0,2,1:T(8,128)} %copy.37, f32[512,8]{0,1:T(8,128)} %get-tuple-element.429), kind=kLoop, calls=%fused_computation.36 | loop fusion | flops 1048576 | bytes 3162112 | tf_op jit(solution)/shard_map/convert_element_type | solution.py:181
  93.8 29.9 %all_to_all.60 = bf16[8,2,32768]{2,1,0:T(2,128)(2,1)S(1)} all-to-all(bf16[8,2,32768]{2,1,0:T(2,128)(2,1)S(1)} %reshape.331), channel_id=1, replica_groups=mesh['groups'=2,'ulysses'=8,'seq'=2] {'ulysses'}, dimensions={0} | all-to-all | bytes 2097152 | tf_op jit(solution)/shard_map/all_to_all | solution.py:184
  (66 shorter events, 28.3 us)
Async XLA Ops:
  0.0 0.9 copy-start
  0.0 36.2 %copy-start.1 = (s32[1024]{0:T(1024)S(1)}, s32[1024]{0:T(1024)}, u32[]{:S(2)}) copy-start(s32[1024]{0:T(1024)} %param.12) | copy-start | bytes 12292
  0.9 37.7 %copy-start.5 = (s32[128]{0:T(128)S(1)}, s32[128]{0:T(128)}, u32[]{:S(2)}) copy-start(s32[128]{0:T(128)} %param.13) | copy-start | bytes 1540
  1.6 14.6 %all-to-all-start = ((bf16[64,8,128]{2,0,1:T(8,128)(2,1)}), bf16[64,8,128]{2,0,1:T(8,128)(2,1)S(1)}, u32[]{:S(2)}, u32[]{:S(2)}) async-start(bf16[64,8,128]{2,0,1:T(8,128)(2,1)} %copy_bitcast_fusion.2), calls=%async_computation | async-start | bytes 262144 | tf_op jit(solution)/shard_map/all_to_all | solution.py:147
  16.2 10.7 %all-to-all-start.2 = ((bf16[64,8,128]{2,0,1:T(8,128)(2,1)}), bf16[64,8,128]{2,0,1:T(8,128)(2,1)S(1)}, u32[]{:S(2)}, u32[]{:S(2)}) async-start(bf16[64,8,128]{2,0,1:T(8,128)(2,1)} %copy_bitcast_fusion.1), calls=%async_computation.2 | async-start | bytes 262144 | tf_op jit(solution)/shard_map/all_to_all | solution.py:150
  26.9 27.2 %all-to-all-start.1 = ((bf16[64,8,1024]{2,0,1:T(8,128)(2,1)}), bf16[64,8,1024]{2,0,1:T(8,128)(2,1)S(1)}, u32[]{:S(2)}, u32[]{:S(2)}) async-start(bf16[64,8,1024]{2,0,1:T(8,128)(2,1)} %bitcast.66), calls=%async_computation.1 | async-start | bytes 2097152 | tf_op jit(solution)/shard_map/all_to_all | solution.py:127
  64.8 3.3 %copy-start.2 = (f32[512,8]{0,1:T(8,128)S(1)}, f32[512,8]{0,1:T(8,128)}, u32[]{:S(2)}) copy-start(f32[512,8]{0,1:T(8,128)} %get-tuple-element.553) | copy-start | bytes 49156 | tf_op jit(solution)/shard_map/while/body/eval_jaxpr/while/body/eval_jaxpr/cond
  64.8 3.3 %copy-start.4 = (bf16[1024,128]{1,0:T(8,128)(2,1)S(1)}, bf16[1024,128]{1,0:T(8,128)(2,1)}, u32[]{:S(2)}) copy-start(bf16[1024,128]{1,0:T(8,128)(2,1)} %get-tuple-element.555) | copy-start | bytes 786436 | tf_op jit(solution)/shard_map/while/body/eval_jaxpr/while/body/eval_jaxpr/cond
  68.1 2.9 %copy-start.3 = (f32[512,8]{0,1:T(8,128)}, f32[512,8]{0,1:T(8,128)S(1)}, u32[]{:S(2)}) copy-start(f32[512,8]{0,1:T(8,128)S(1)} %get-tuple-element.726) | copy-start | bytes 49156 | tf_op jit(solution)/shard_map/while/body/eval_jaxpr/while/body/eval_jaxpr/cond
  80.6 3.3 %copy-start.2 = (f32[512,8]{0,1:T(8,128)S(1)}, f32[512,8]{0,1:T(8,128)}, u32[]{:S(2)}) copy-start(f32[512,8]{0,1:T(8,128)} %get-tuple-element.553) | copy-start | bytes 49156 | tf_op jit(solution)/shard_map/while/body/eval_jaxpr/while/body/eval_jaxpr/cond
  80.6 3.3 %copy-start.4 = (bf16[1024,128]{1,0:T(8,128)(2,1)S(1)}, bf16[1024,128]{1,0:T(8,128)(2,1)}, u32[]{:S(2)}) copy-start(bf16[1024,128]{1,0:T(8,128)(2,1)} %get-tuple-element.555) | copy-start | bytes 786436 | tf_op jit(solution)/shard_map/while/body/eval_jaxpr/while/body/eval_jaxpr/cond
  83.9 2.9 %copy-start.3 = (f32[512,8]{0,1:T(8,128)}, f32[512,8]{0,1:T(8,128)S(1)}, u32[]{:S(2)}) copy-start(f32[512,8]{0,1:T(8,128)S(1)} %get-tuple-element.726) | copy-start | bytes 49156 | tf_op jit(solution)/shard_map/while/body/eval_jaxpr/while/body/eval_jaxpr/cond
where the time goes:
time: 127 us; the launch traced here: 126 us
  local copies, waits for them, and re-layouts  34.1 us (27%)
  blocking collectives  34 us (27%)
  other arithmetic  19.5 us (15%)
  starting transfers between devices  14.2 us (11%)
  waiting for transfers between devices  12.6 us (10%)
  matrix products  8.7 us (7%)
  loops' own time  2.94 us (2%)
    all_to_all x1, blocking collectives, shards(): lax.all_to_all(result, 'ulysses', split_axis=0, concat_axis=1, tiled=True)  29.9 us
    all_to_all x1, starting transfers between devices, shards(): lax.all_to_all(spread(key_states, ulysses_count), 'ulysses', split_axis=1...  7.28 us
    gather x1, local copies, waits for them, and re-layouts, shards(): jnp.take(judged, key_place)  6.8 us
    all_to_all x1, waiting for transfers between devices, shards(): lax.all_to_all(spread(key_states, ulysses_count), 'ulysses', split_axis=1...  5.76 us
    gather x1, local copies, waits for them, and re-layouts, shards(): jnp.take(turn_ids, key_place)  5.72 us
    dot_general x2, matrix products, absorb(): jnp.einsum('qhk,kd->qhd', weights.astype(jnp.bfloat16), values_block, pre...  5.69 us
    unnamed x13, local copies, waits for them, and re-layouts  5.12 us
    all_to_all x1, waiting for transfers between devices, shards(): lax.all_to_all(spread(value_states, ulysses_count), 'ulysses', split_axis...  4.99 us
  transfers between devices with their start and end apart: 3, of which 3 were waited for; matrix products, arithmetic and copies ran while one was open for 17% of the time, Pallas kernels for 0%

commit v1 on v0

--- a/solution.py
+++ b/solution.py
@@ -6,6 +6,17 @@
 
 HEAD_DIM = 128
 floor_score = -1e30
+
+
+def _lead_sectors(z_in, out_dim, work_x):
+    piece_out, parts_out = (z_in.shape[:out_dim], z_in.shape[out_dim + 1 :])
+    return jnp.moveaxis(z_in.reshape(*piece_out, work_x, -1, *parts_out), out_dim, 0)
+
+
+def spot_cut(arr, dim_at):
+    left_arr = list(arr.shape[1:])
+    left_arr[dim_at] *= arr.shape[0]
+    return jnp.moveaxis(arr, 0, dim_at).reshape(left_arr)
 
 
 def absorb(
@@ -181,7 +192,17 @@
         .astype(jnp.bfloat16)
         .reshape(query_total, 1, heads_here * HEAD_DIM)
     )
-    returned = lax.all_to_all(result, "ulysses", split_axis=0, concat_axis=1, tiled=True)
+    field_out = lax.axis_size("ulysses")
+    even = lax.axis_index("ulysses")
+    then, mid_arr = (field_out, even)
+    q_next = _lead_sectors(result, 0, then)
+    runs = [q_next[mid_arr]]
+    for m in [*range(1, then)]:
+        r1 = q_next[mid_arr ^ m]
+        g_now = lax.ppermute(r1, axis_name="ulysses", perm=[(ix, ix ^ m) for ix in range(then)])
+        runs.append(g_now)
+    q_next = jnp.stack(runs)[mid_arr ^ jnp.arange(then)]
+    returned = spot_cut(q_next, 1)
     return returned.reshape(tokens_here, ulysses_count * heads_here * HEAD_DIM)
 
 

time: 127 us -> 119 us (0.937); the launches traced: 126 us -> 117 us
  blocking collectives: 34 us -> 4.1 us
  waiting for transfers between devices: 12.6 us -> 26.7 us
  starting transfers between devices: 14.2 us -> 25.7 us
  local copies, waits for them, and re-layouts: 34.1 us -> 30.9 us
  other arithmetic: 19.5 us -> 17.5 us
    all_to_all x1 -> x0, blocking collectives: 29.9 us -> none  [shards(): lax.all_to_all(result, 'ulysses', split_axis=0, concat_axis=1, tiled=True)]
    ppermute x0 -> x7, waiting for transfers between devices: none -> 14.1 us  [shards(): lax.ppermute(r1, axis_name='ulysses', perm=[(ix, ix ^ m) for ix in range(...]
    ppermute x0 -> x7, starting transfers between devices: none -> 11.5 us  [shards(): lax.ppermute(r1, axis_name='ulysses', perm=[(ix, ix ^ m) for ix in range(...]
    unnamed x13 -> x15, local copies, waits for them, and re-layouts: 5.12 us -> 2.44 us
    while x1 -> x0, local copies, waits for them, and re-layouts: 1.85 us -> none  [over_queries(): window = lax.fori_loop(0, key_count // key_step, over_keys, window)]
    reshape x1 -> x0, other arithmetic: 1.45 us -> none  [shards(): result = (running / totals[:, :, None]).astype(jnp.bfloat16).reshape(quer...]
  transfers between devices with their start and end apart: 3 -> 10, of which waited for: 3 -> 7; matrix products, arithmetic and copies ran while one was open for 17% -> 18% of each run, Pallas kernels for 0% -> 0%
where the time goes in v1:
time: 119 us; the launch traced here: 117 us
  local copies, waits for them, and re-layouts  30.9 us (26%)
  waiting for transfers between devices  26.7 us (22%)
  starting transfers between devices  25.7 us (22%)
  other arithmetic  17.5 us (15%)
  matrix products  8.69 us (7%)
  blocking collectives  4.1 us (3%)
  loops' own time  2.67 us (2%)
    ppermute x7, waiting for transfers between devices, shards(): lax.ppermute(r1, axis_name='ulysses', perm=[(ix, ix ^ m) for ix in range(...  14.1 us
    ppermute x7, starting transfers between devices, shards(): lax.ppermute(r1, axis_name='ulysses', perm=[(ix, ix ^ m) for ix in range(...  11.5 us
    all_to_all x1, starting transfers between devices, shards(): lax.all_to_all(spread(key_states, ulysses_count), 'ulysses', split_axis=1...  7.28 us
    gather x1, local copies, waits for them, and re-layouts, shards(): jnp.take(judged, key_place)  6.8 us
    all_to_all x1, waiting for transfers between devices, shards(): lax.all_to_all(spread(key_states, ulysses_count), 'ulysses', split_axis=1...  5.76 us
    gather x1, local copies, waits for them, and re-layouts, shards(): jnp.take(turn_ids, key_place)  5.72 us
    dot_general x2, matrix products, absorb(): jnp.einsum('qhk,kd->qhd', weights.astype(jnp.bfloat16), values_block, pre...  5.68 us
    all_to_all x1, waiting for transfers between devices, shards(): lax.all_to_all(spread(value_states, ulysses_count), 'ulysses', split_axis...  4.99 us
  transfers between devices with their start and end apart: 10, of which 7 were waited for; matrix products, arithmetic and copies ran while one was open for 18% of the time, Pallas kernels for 0%

profile of v1, /device:TPU:0, one launch (start us, length us, event | category | flops | bytes accessed | tf_op | source)
XLA Modules:
  0.0 116.6 jit_solution(6946670938973504655)
XLA Ops:
  1.6 7.3 %all-to-all-start = ((bf16[64,8,128]{2,0,1:T(8,128)(2,1)}), bf16[64,8,128]{2,0,1:T(8,128)(2,1)S(1)}, u32[]{:S(2)}, u32[]{:S(2)}) async-start(bf16[64,8,128]{2,0,1:T(8,128)(2,1)} %copy_bitcast_fusion.2), calls=%async_computation | async-start | bytes 262144 | tf_op jit(solution)/shard_map/all_to_all | solution.py:158
  10.5 5.8 %all-to-all-done = bf16[64,8,128]{2,0,1:T(8,128)(2,1)S(1)} async-done(((bf16[64,8,128]{2,0,1:T(8,128)(2,1)}), bf16[64,8,128]{2,0,1:T(8,128)(2,1)S(1)}, u32[]{:S(2)}, u32[]{:S(2)}) %all-to-all-start) | async-done | bytes 131104 | tf_op jit(solution)/shard_map/all_to_all | solution.py:158
  16.2 3.4 %all-to-all-start.2 = ((bf16[64,8,128]{2,0,1:T(8,128)(2,1)}), bf16[64,8,128]{2,0,1:T(8,128)(2,1)S(1)}, u32[]{:S(2)}, u32[]{:S(2)}) async-start(bf16[64,8,128]{2,0,1:T(8,128)(2,1)} %copy_bitcast_fusion.1), calls=%async_computation.2 | async-start | bytes 262144 | tf_op jit(solution)/shard_map/all_to_all | solution.py:161
  19.6 2.3 %copy.60 = bf16[8,8,8,1024]{3,2,0,1:T(8,128)(2,1)} copy(bf16[8,8,8,1024]{3,2,1,0:T(8,128)(2,1)} %bitcast.115) | data formatting | bytes 2097152 | tf_op jit(solution)/shard_map/reshape | solution.py:139
  21.9 5.0 %all-to-all-done.2 = bf16[64,8,128]{2,0,1:T(8,128)(2,1)S(1)} async-done(((bf16[64,8,128]{2,0,1:T(8,128)(2,1)}), bf16[64,8,128]{2,0,1:T(8,128)(2,1)S(1)}, u32[]{:S(2)}, u32[]{:S(2)}) %all-to-all-start.2) | async-done | bytes 131104 | tf_op jit(solution)/shard_map/all_to_all | solution.py:161
  26.9 3.6 %all-to-all-start.1 = ((bf16[64,8,1024]{2,0,1:T(8,128)(2,1)}), bf16[64,8,1024]{2,0,1:T(8,128)(2,1)S(1)}, u32[]{:S(2)}, u32[]{:S(2)}) async-start(bf16[64,8,1024]{2,0,1:T(8,128)(2,1)} %bitcast.110), calls=%async_computation.1 | async-start | bytes 2097152 | tf_op jit(solution)/shard_map/all_to_all | solution.py:138
  30.5 5.7 %gather_fusion = s32[1024]{0:T(1024)S(1)} fusion(s32[1024]{0:T(1024)} %param.12, s32[1024]{0:T(1024)S(1)} %broadcast_clamp_fusion), kind=kCustom, calls=%fused_computation | custom fusion | bytes 12288 | tf_op jit(solution)/shard_map/jit(_take)/gather | solution.py:186
  36.3 2.3 %gather_fusion.1 = s32[512]{0:T(512)S(1)} fusion(s32[1024]{0:T(1024)S(1)} %copy-done.1, s32[1024]{0:T(1024)S(1)} %pad_clamp_fusion.1), kind=kCustom, calls=%fused_computation.1 | custom fusion | bytes 6144 | tf_op jit(solution)/shard_map/jit(_take)/gather | solution.py:151
  38.8 6.8 %gather_fusion.2 = pred[1024]{0:T(1024)(128)(4,1)S(1)} fusion(pred[1024]{0:T(1024)(128)(4,1)S(1)} %fusion.24, s32[1024]{0:T(1024)S(1)} %broadcast_clamp_fusion), kind=kCustom, calls=%fused_computation.2 | custom fusion | bytes 6144 | tf_op jit(solution)/shard_map/jit(_take)/gather | solution.py:187
  48.1 2.0 %all_gather.6 = bf16[1024,128]{1,0:T(8,128)(2,1)S(1)} all-gather(bf16[512,128]{1,0:T(8,128)(2,1)S(1)} %bitcast.116), channel_id=1, replica_groups=mesh['groups'=2,'ulysses'=8,'seq'=2] {'seq'}, dimensions={0}, use_global_device_ids=true | all-gather | bytes 393216 | tf_op jit(solution)/shard_map/all_gather | solution.py:168
  50.1 2.1 %all_gather.7 = bf16[1024,128]{1,0:T(8,128)(2,1)} all-gather(bf16[512,128]{1,0:T(8,128)(2,1)S(1)} %bitcast.117), channel_id=1, replica_groups=mesh['groups'=2,'ulysses'=8,'seq'=2] {'seq'}, dimensions={0}, use_global_device_ids=true | all-gather | bytes 393216 | tf_op jit(solution)/shard_map/all_gather | solution.py:169
  55.2 31.2 %while.31 = (s32[]{:T(128)}, f32[512,8]{0,1:T(8,128)S(1)}, f32[512,8]{0,1:T(8,128)}, f32[512,8,128]{2,0,1:T(8,128)S(1)}, s32[1024]{0:T(1024)}, /*index=5*/s32[]{...) while((s32[]{:T(128)}, f32[512,8]{0,1:T(8,128)S(1)}, ...), condition=%wide.region_8.9_spmd.clone, body=%wide.region_2.8_spmd.clone.sunk | while | flops 1098925056 | bytes 33209420 | solution.py:107
  55.2 2.0 %fusion.68 = (s32[]{:T(128)}, s32[512]{0:T(512)}) fusion(s32[1024]{0:T(1024)} %get-tuple-element.763, s32[]{:T(128)} %select_n.437), kind=kLoop, calls=%fused_computation.136.clone.1 | loop fusion | flops 511 | bytes 4104 | tf_op jit(solution)/shard_map/while/body/eval_jaxpr/while/body/eval_jaxpr/reduce_min | solution.py:90
  61.3 9.5 %conditional.3 = ((f32[512,8]{0,1:T(8,128)S(1)}, f32[512,8]{0,1:T(8,128)}, f32[512,8,128]{2,0,1:T(8,128)S(1)})) conditional(s32[]{:T(128)} %convert_element_type.25, (f32[512,8]{0,1:T(8,128)S(1)}, f32[512,8]{0,1:T(8,128)}, f32[512,8,128]{2,0,1:T(8,128)S(1)}) %tuple.82, (s32[512]{0:T(512)}, s32[512]{0:T(512)}, s32[1024]{0:T(1024)}, s32[]{:T(128)}, ...), branch_computations={%region_4.4_spmd, %region_5.7_spmd.clone} | conditional | flops 1098922496 | bytes 33194124 | solution.py:89
  68.0 2.8 %multiply_add_fusion = f32[512,8,128]{2,0,1:T(8,128)S(1)} fusion(f32[512,8,128]{2,0,1:T(8,128)S(1)} %get-tuple-element.541, f32[512,512,8]{1,0,2:T(8,128)S(1)} %get-tuple-element.609, f32[512,8]{0,1:T(8,128)S(1)} %max.5, pred[512,512]{0,1:T(8,128)(4,1)S(1)} %or_and_fusion, f32[512,8]{0,1:T(8,128)S(1)} %get-tuple-element.605, ...), kind=kOutput, calls=%fused_computation.12 | convolution fusion | flops 546308096 | bytes 13008900 | tf_op jit(solution)/shard_map/while/body/eval_jaxpr/while/body/eval_jaxpr/cond/branch_1_fun/qhk,kd->qhd/dot_general | solution.py:47
  70.9 2.0 %fusion.68 = (s32[]{:T(128)}, s32[512]{0:T(512)}) fusion(s32[1024]{0:T(1024)} %get-tuple-element.763, s32[]{:T(128)} %select_n.437), kind=kLoop, calls=%fused_computation.136.clone.1 | loop fusion | flops 511 | bytes 4104 | tf_op jit(solution)/shard_map/while/body/eval_jaxpr/while/body/eval_jaxpr/reduce_min | solution.py:90
  76.9 9.5 %conditional.3 = ((f32[512,8]{0,1:T(8,128)S(1)}, f32[512,8]{0,1:T(8,128)}, f32[512,8,128]{2,0,1:T(8,128)S(1)})) conditional(s32[]{:T(128)} %convert_element_type.25, (f32[512,8]{0,1:T(8,128)S(1)}, f32[512,8]{0,1:T(8,128)}, f32[512,8,128]{2,0,1:T(8,128)S(1)}) %tuple.82, (s32[512]{0:T(512)}, s32[512]{0:T(512)}, s32[1024]{0:T(1024)}, s32[]{:T(128)}, ...), branch_computations={%region_4.4_spmd, %region_5.7_spmd.clone} | conditional | flops 1098922496 | bytes 33194124 | solution.py:89
  83.6 2.8 %multiply_add_fusion = f32[512,8,128]{2,0,1:T(8,128)S(1)} fusion(f32[512,8,128]{2,0,1:T(8,128)S(1)} %get-tuple-element.541, f32[512,512,8]{1,0,2:T(8,128)S(1)} %get-tuple-element.609, f32[512,8]{0,1:T(8,128)S(1)} %max.5, pred[512,512]{0,1:T(8,128)(4,1)S(1)} %or_and_fusion, f32[512,8]{0,1:T(8,128)S(1)} %get-tuple-element.605, ...), kind=kOutput, calls=%fused_computation.12 | convolution fusion | flops 546308096 | bytes 13008900 | tf_op jit(solution)/shard_map/while/body/eval_jaxpr/while/body/eval_jaxpr/cond/branch_1_fun/qhk,kd->qhd/dot_general | solution.py:47
  90.9 2.0 %collective-permute-start.2 = (bf16[64,1,1024]{2,0,1:T(8,128)(2,1)S(1)}, bf16[64,1,1024]{2,0,1:T(8,128)(2,1)S(1)}, u32[]{:S(2)}, u32[]{:S(2)}) collective-permute-start(bf16[64,1,1024]{2,0,1:T(8,128)(2,1)S(1)} %get-tuple-element.616), channel_id=1, source_target_pairs={{0,6},{2,4},{4,2},{6,0},{8,14},{10,12},{12,10},{14,8},{1,7},{3,5},... | collective-permute-start | bytes 393224 | tf_op jit(solution)/shard_map/ppermute | solution.py:202
  93.8 2.6 %collective-permute-start.4 = (bf16[64,1,1024]{2,0,1:T(8,128)(2,1)S(1)}, bf16[64,1,1024]{2,0,1:T(8,128)(2,1)S(1)}, u32[]{:S(2)}, u32[]{:S(2)}) collective-permute-start(bf16[64,1,1024]{2,0,1:T(8,128)(2,1)S(1)} %get-tuple-element.614), channel_id=1, source_target_pairs={{0,10},{2,8},{4,14},{6,12},{8,2},{10,0},{12,6},{14,4},{1,11},{3,9}... | collective-permute-start | bytes 393224 | tf_op jit(solution)/shard_map/ppermute | solution.py:202
  96.5 2.1 %collective-permute-start.5 = (bf16[64,1,1024]{2,0,1:T(8,128)(2,1)S(1)}, bf16[64,1,1024]{2,0,1:T(8,128)(2,1)S(1)}, u32[]{:S(2)}, u32[]{:S(2)}) collective-permute-start(bf16[64,1,1024]{2,0,1:T(8,128)(2,1)S(1)} %get-tuple-element.613), channel_id=1, source_target_pairs={{0,12},{2,14},{4,8},{6,10},{8,4},{10,6},{12,0},{14,2},{1,13},{3,15... | collective-permute-start | bytes 393224 | tf_op jit(solution)/shard_map/ppermute | solution.py:202
  98.6 2.2 %collective-permute-start.6 = (bf16[64,1,1024]{2,0,1:T(8,128)(2,1)S(1)}, bf16[64,1,1024]{2,0,1:T(8,128)(2,1)S(1)}, u32[]{:S(2)}, u32[]{:S(2)}) collective-permute-start(bf16[64,1,1024]{2,0,1:T(8,128)(2,1)S(1)} %get-tuple-element.612), channel_id=1, source_target_pairs={{0,14},{2,12},{4,10},{6,8},{8,6},{10,4},{12,2},{14,0},{1,15},{3,13... | collective-permute-start | bytes 393224 | tf_op jit(solution)/shard_map/ppermute | solution.py:202
  101.7 9.7 %collective-permute-done.3 = bf16[64,1,1024]{2,0,1:T(8,128)(2,1)S(1)} collective-permute-done((bf16[64,1,1024]{2,0,1:T(8,128)(2,1)S(1)}, bf16[64,1,1024]{2,0,1:T(8,128)(2,1)S(1)}, u32[]{:S(2)}, u32[]{:S(2)}) %collective-permute-start.3) | collective-permute-done | bytes 131104 | tf_op jit(solution)/shard_map/ppermute | solution.py:202
  111.4 3.5 %collective-permute-done.4 = bf16[64,1,1024]{2,0,1:T(8,128)(2,1)S(1)} collective-permute-done((bf16[64,1,1024]{2,0,1:T(8,128)(2,1)S(1)}, bf16[64,1,1024]{2,0,1:T(8,128)(2,1)S(1)}, u32[]{:S(2)}, u32[]{:S(2)}) %collective-permute-start.4) | collective-permute-done | bytes 131104 | tf_op jit(solution)/shard_map/ppermute | solution.py:202
  (85 shorter events, 35.8 us)
Async XLA Ops:
  0.0 0.9 copy-start
  0.0 36.3 %copy-start.1 = (s32[1024]{0:T(1024)S(1)}, s32[1024]{0:T(1024)}, u32[]{:S(2)}) copy-start(s32[1024]{0:T(1024)} %param.12) | copy-start | bytes 12292
  0.9 37.7 %copy-start.5 = (s32[128]{0:T(128)S(1)}, s32[128]{0:T(128)}, u32[]{:S(2)}) copy-start(s32[128]{0:T(128)} %param.13) | copy-start | bytes 1540
  1.6 14.6 %all-to-all-start = ((bf16[64,8,128]{2,0,1:T(8,128)(2,1)}), bf16[64,8,128]{2,0,1:T(8,128)(2,1)S(1)}, u32[]{:S(2)}, u32[]{:S(2)}) async-start(bf16[64,8,128]{2,0,1:T(8,128)(2,1)} %copy_bitcast_fusion.2), calls=%async_computation | async-start | bytes 262144 | tf_op jit(solution)/shard_map/all_to_all | solution.py:158
  16.2 10.7 %all-to-all-start.2 = ((bf16[64,8,128]{2,0,1:T(8,128)(2,1)}), bf16[64,8,128]{2,0,1:T(8,128)(2,1)S(1)}, u32[]{:S(2)}, u32[]{:S(2)}) async-start(bf16[64,8,128]{2,0,1:T(8,128)(2,1)} %copy_bitcast_fusion.1), calls=%async_computation.2 | async-start | bytes 262144 | tf_op jit(solution)/shard_map/all_to_all | solution.py:161
  26.9 27.2 %all-to-all-start.1 = ((bf16[64,8,1024]{2,0,1:T(8,128)(2,1)}), bf16[64,8,1024]{2,0,1:T(8,128)(2,1)S(1)}, u32[]{:S(2)}, u32[]{:S(2)}) async-start(bf16[64,8,1024]{2,0,1:T(8,128)(2,1)} %bitcast.110), calls=%async_computation.1 | async-start | bytes 2097152 | tf_op jit(solution)/shard_map/all_to_all | solution.py:138
  64.6 3.3 %copy-start.2 = (f32[512,8]{0,1:T(8,128)S(1)}, f32[512,8]{0,1:T(8,128)}, u32[]{:S(2)}) copy-start(f32[512,8]{0,1:T(8,128)} %get-tuple-element.540) | copy-start | bytes 49156 | tf_op jit(solution)/shard_map/while/body/eval_jaxpr/while/body/eval_jaxpr/cond
  64.6 3.3 %copy-start.4 = (bf16[1024,128]{1,0:T(8,128)(2,1)S(1)}, bf16[1024,128]{1,0:T(8,128)(2,1)}, u32[]{:S(2)}) copy-start(bf16[1024,128]{1,0:T(8,128)(2,1)} %get-tuple-element.542) | copy-start | bytes 786436 | tf_op jit(solution)/shard_map/while/body/eval_jaxpr/while/body/eval_jaxpr/cond
  67.9 2.9 %copy-start.3 = (f32[512,8]{0,1:T(8,128)}, f32[512,8]{0,1:T(8,128)S(1)}, u32[]{:S(2)}) copy-start(f32[512,8]{0,1:T(8,128)S(1)} %get-tuple-element.721) | copy-start | bytes 49156 | tf_op jit(solution)/shard_map/while/body/eval_jaxpr/while/body/eval_jaxpr/cond
  80.2 3.3 %copy-start.2 = (f32[512,8]{0,1:T(8,128)S(1)}, f32[512,8]{0,1:T(8,128)}, u32[]{:S(2)}) copy-start(f32[512,8]{0,1:T(8,128)} %get-tuple-element.540) | copy-start | bytes 49156 | tf_op jit(solution)/shard_map/while/body/eval_jaxpr/while/body/eval_jaxpr/cond
  80.2 3.3 %copy-start.4 = (bf16[1024,128]{1,0:T(8,128)(2,1)S(1)}, bf16[1024,128]{1,0:T(8,128)(2,1)}, u32[]{:S(2)}) copy-start(bf16[1024,128]{1,0:T(8,128)(2,1)} %get-tuple-element.542) | copy-start | bytes 786436 | tf_op jit(solution)/shard_map/while/body/eval_jaxpr/while/body/eval_jaxpr/cond
  83.6 2.9 %copy-start.3 = (f32[512,8]{0,1:T(8,128)}, f32[512,8]{0,1:T(8,128)S(1)}, u32[]{:S(2)}) copy-start(f32[512,8]{0,1:T(8,128)S(1)} %get-tuple-element.721) | copy-start | bytes 49156 | tf_op jit(solution)/shard_map/while/body/eval_jaxpr/while/body/eval_jaxpr/cond
  89.2 7.2 %collective-permute-start = (bf16[64,1,1024]{2,0,1:T(8,128)(2,1)S(1)}, bf16[64,1,1024]{2,0,1:T(8,128)(2,1)S(1)}, u32[]{:S(2)}, u32[]{:S(2)}) collective-permute-start(bf16[64,1,1024]{2,0,1:T(8,128)(2,1)S(1)} %get-tuple-element.618), channel_id=1, source_target_pairs={{0,2},{2,0},{4,6},{6,4},{8,10},{10,8},{12,14},{14,12},{1,3},{3,1},... | collective-permute-start | bytes 393224 | tf_op jit(solution)/shard_map/ppermute | solution.py:202
  90.5 8.1 %collective-permute-start.1 = (bf16[64,1,1024]{2,0,1:T(8,128)(2,1)S(1)}, bf16[64,1,1024]{2,0,1:T(8,128)(2,1)S(1)}, u32[]{:S(2)}, u32[]{:S(2)}) collective-permute-start(bf16[64,1,1024]{2,0,1:T(8,128)(2,1)S(1)} %get-tuple-element.617), channel_id=1, source_target_pairs={{0,4},{2,6},{4,0},{6,2},{8,12},{10,14},{12,8},{14,10},{1,5},{3,7},... | collective-permute-start | bytes 393224 | tf_op jit(solution)/shard_map/ppermute | solution.py:202
  90.9 10.8 %collective-permute-start.2 = (bf16[64,1,1024]{2,0,1:T(8,128)(2,1)S(1)}, bf16[64,1,1024]{2,0,1:T(8,128)(2,1)S(1)}, u32[]{:S(2)}, u32[]{:S(2)}) collective-permute-start(bf16[64,1,1024]{2,0,1:T(8,128)(2,1)S(1)} %get-tuple-element.616), channel_id=1, source_target_pairs={{0,6},{2,4},{4,2},{6,0},{8,14},{10,12},{12,10},{14,8},{1,7},{3,5},... | collective-permute-start | bytes 393224 | tf_op jit(solution)/shard_map/ppermute | solution.py:202
  92.8 18.5 %collective-permute-start.3 = (bf16[64,1,1024]{2,0,1:T(8,128)(2,1)S(1)}, bf16[64,1,1024]{2,0,1:T(8,128)(2,1)S(1)}, u32[]{:S(2)}, u32[]{:S(2)}) collective-permute-start(bf16[64,1,1024]{2,0,1:T(8,128)(2,1)S(1)} %get-tuple-element.615), channel_id=1, source_target_pairs={{0,8},{2,10},{4,12},{6,14},{8,0},{10,2},{12,4},{14,6},{1,9},{3,11}... | collective-permute-start | bytes 393224 | tf_op jit(solution)/shard_map/ppermute | solution.py:202
  93.8 21.1 %collective-permute-start.4 = (bf16[64,1,1024]{2,0,1:T(8,128)(2,1)S(1)}, bf16[64,1,1024]{2,0,1:T(8,128)(2,1)S(1)}, u32[]{:S(2)}, u32[]{:S(2)}) collective-permute-start(bf16[64,1,1024]{2,0,1:T(8,128)(2,1)S(1)} %get-tuple-element.614), channel_id=1, source_target_pairs={{0,10},{2,8},{4,14},{6,12},{8,2},{10,0},{12,6},{14,4},{1,11},{3,9}... | collective-permute-start | bytes 393224 | tf_op jit(solution)/shard_map/ppermute | solution.py:202
  96.5 18.4 %collective-permute-start.5 = (bf16[64,1,1024]{2,0,1:T(8,128)(2,1)S(1)}, bf16[64,1,1024]{2,0,1:T(8,128)(2,1)S(1)}, u32[]{:S(2)}, u32[]{:S(2)}) collective-permute-start(bf16[64,1,1024]{2,0,1:T(8,128)(2,1)S(1)} %get-tuple-element.613), channel_id=1, source_target_pairs={{0,12},{2,14},{4,8},{6,10},{8,4},{10,6},{12,0},{14,2},{1,13},{3,15... | collective-permute-start | bytes 393224 | tf_op jit(solution)/shard_map/ppermute | solution.py:202
  98.6 16.3 %collective-permute-start.6 = (bf16[64,1,1024]{2,0,1:T(8,128)(2,1)S(1)}, bf16[64,1,1024]{2,0,1:T(8,128)(2,1)S(1)}, u32[]{:S(2)}, u32[]{:S(2)}) collective-permute-start(bf16[64,1,1024]{2,0,1:T(8,128)(2,1)S(1)} %get-tuple-element.612), channel_id=1, source_target_pairs={{0,14},{2,12},{4,10},{6,8},{8,6},{10,4},{12,2},{14,0},{1,15},{3,13... | collective-permute-start | bytes 393224 | tf_op jit(solution)/shard_map/ppermute | solution.py:202
